TPU v7x, 256 devices: a whole 4x4x8 slice. The times are simulated.
256 devices in a mesh: dp: 128 (over z, y, x), sub: 2 (over core).
Axes of the slice: x: 4, y: 4, z: 8, core: 2. Of those that a mesh axis runs over, the one named last changes fastest.
Arguments:
- grads: bfloat16 [128, 2, 2048, 512], P('dp', None, 'sub'), may hold values from -84 to 84
- errors: bfloat16 [128, 2, 2048, 512], P('dp', None, 'sub'), may hold values from -3 to 3
- vec_grads: float32 [128, 2, 2048], P('dp', None, 'sub'), may hold values from -24 to 24
- gains: float32 [2, 2048], P(None, 'sub'), may hold values from 0.5 to 1.5
- q_start: float32 [2, 512, 32], replicated, may hold values from -0.25 to 0.25
- owner: int32 [256], replicated, may hold values from 0 to 127, as said below
- momentum: float32 [512, 16, 512], P('dp', None, 'sub'), may hold values from -3 to 3
- master: float32 [512, 16, 512], P('dp', None, 'sub'), may hold values from -5 to 5
Outputs:
- errors_out: bfloat16 [128, 2, 2048, 512], P('dp', None, 'sub')
- new_gains: float32 [2, 2048], P(None, 'sub')
- new_momentum: float32 [512, 16, 512], P('dp', None, 'sub')
- new_master: float32 [512, 16, 512], P('dp', None, 'sub')
- weights: bfloat16 [2, 2048, 512], P(None, None, 'sub')
Inputs may be any that keep to these rules, and one draw needn't show every extreme that they name: `owner`: each dp index owns at most 4 blocks and some index owns exactly 4; momentum and master in empty slots are not used.
All inputs are finite; a program needn't handle non-finite values.
Results may differ from a plain program's by a relative error of at most 0.005.
Values may be sent and summed in bfloat16 or wider, within the bound.
A program may use at most 128 MiB of HBM per device.

v0:
```python
import jax
import jax.numpy as jnp
from jax import lax
from jax.sharding import PartitionSpec as P

ROUNDS = 2
HIGH = lax.Precision.HIGHEST
momentum_decay = 0.9
step_rate = 0.5
vector_rate = 1.0


def solve_basis(left, gram):
    lower = jnp.linalg.cholesky(gram)
    return lax.linalg.triangular_solve(lower, left, left_side=False, lower=True, transpose_a=True)


def body(grads, errors, vec_grads, gains, q_start, owner, momentum, master):
    replicas = lax.axis_size("dp")
    slots = momentum.shape[0]
    rows_block = momentum.shape[1]
    half_cols = momentum.shape[2]
    blocks = owner.shape[0]
    mixed = grads[0].astype(jnp.float32) + errors[0].astype(jnp.float32)
    mats = mixed.shape[0]
    vec_total = lax.psum(vec_grads[0], "dp")
    new_gains = gains - vector_rate * (vec_total / replicas)
    right = q_start
    for step_index in range(ROUNDS):
        local_left = jnp.einsum("mdk,mkr->mdr", mixed, right, precision=HIGH)
        left = lax.psum(local_left, "dp") / replicas
        gram = lax.psum(jnp.einsum("mdr,mds->mrs", left, left, precision=HIGH), "sub")
        basis = solve_basis(left, gram)
        local_right = jnp.einsum("mdk,mdr->mkr", mixed, basis, precision=HIGH)
        right = lax.psum(local_right, ("dp", "sub")) / replicas
    approx_local = jnp.einsum("mdr,mkr->mdk", basis, right, precision=HIGH)
    errors_out = (mixed - approx_local).astype(jnp.bfloat16)[None]
    basis_full = lax.all_gather(basis.astype(jnp.bfloat16), "sub", axis=1, tiled=True).astype(
        basis.dtype
    )
    right_half = lax.dynamic_slice_in_dim(right, lax.axis_index("sub") * half_cols, half_cols, 1)
    approx_half = jnp.einsum("mdr,mkr->mdk", basis_full, right_half, precision=HIGH)
    full_rows = basis_full.shape[1]
    approx_blocks = approx_half.reshape(blocks, rows_block, half_cols)
    index = jnp.arange(blocks, dtype=jnp.int32)
    same = owner[:, None] == owner[None, :]
    earlier = index[None, :] < index[:, None]
    rank = jnp.sum((same & earlier).astype(jnp.int32), axis=1)
    pos = owner * slots + rank
    mine = (owner[None, :] == lax.axis_index("dp")) & (
        rank[None, :] == jnp.arange(slots, dtype=jnp.int32)[:, None]
    )
    mine_int = mine.astype(jnp.int32)
    local_block = jnp.sum(mine_int * index[None, :], axis=1)
    valid = jnp.sum(mine_int, axis=1).astype(jnp.float32)[:, None, None]
    approx_slots = approx_blocks[local_block] * valid
    new_momentum = (momentum_decay * momentum + approx_slots) * valid
    new_master = (master - step_rate * new_momentum) * valid
    gathered = lax.all_gather(new_master.astype(jnp.bfloat16), "dp", axis=0, tiled=True)
    weights = gathered[pos].reshape(mats, full_rows, half_cols)
    return (errors_out, new_gains, new_momentum, new_master, weights)


def solution(mesh):
    placed = (
        P("dp", None, "sub", None),
        P("dp", None, "sub", None),
        P("dp", None, "sub"),
        P(None, "sub"),
        P(),
        P(),
        P("dp", None, "sub"),
        P("dp", None, "sub"),
    )
    return jax.shard_map(
        body,
        mesh=mesh,
        in_specs=placed,
        out_specs=(
            P("dp", None, "sub", None),
            P(None, "sub"),
            P("dp", None, "sub"),
            P("dp", None, "sub"),
            P(None, None, "sub"),
        ),
        check_vma=False,
    )
```

profile of v0, /device:TPU:2, one launch (start us, length us, event | category | flops | bytes accessed | tf_op | source)
XLA Modules:
  0.0 1345.0 jit_solution(2822538106656851169)
XLA Ops:
  7.2 0.0 copy-start
  7.2 0.0 all-reduce.5.cloned.1.call-start
  7.2 0.8 copy-done
  8.1 7.2 fusion.6
  15.3 0.0 all-reduce.5.cloned.1.call-update
  15.3 0.0 all-reduce.7.cloned.1.call-start
  15.4 0.2 convert_reduce_fusion
  15.6 215.6 %all-reduce.5.cloned.1.call-done = f32[2,1024,32]{1,2,0:T(8,128)} async-done(((f32[2,1024,32]{1,2,0:T(8,128)}), f32[2,1024,32]{1,2,0:T(8,128)}) %all-reduce.5.cloned.1.call-update) | async-done | bytes 262160 | tf_op jit(solution)/shard_map/psum | solution.py:31
  231.1 1.4 fusion.15
  232.5 3.4 psum.50
  236.0 0.1 copy.30
  236.0 5.9 custom-call.8
  241.9 0.1 compare_reduce_fusion.1
  242.1 0.1 select_bitcast_fusion.1
  242.1 4.9 custom-call.9
  247.1 1.4 convolution_bitcast_fusion.1
  248.5 5.2 fusion.4
  253.7 0.0 all-reduce.7.cloned.1.call-update
  253.7 0.0 all-reduce.9.cloned.1.call-start
  253.8 0.1 convert_reduce_fusion.1
  253.9 239.2 %all-reduce.7.cloned.1.call-done = f32[2,512,32]{1,2,0:T(8,128)} async-done(((f32[2,512,32]{1,2,0:T(8,128)}), f32[2,512,32]{1,2,0:T(8,128)}) %all-reduce.7.cloned.1.call-update) | async-done | bytes 131088 | tf_op jit(solution)/shard_map/psum | solution.py:35
  493.1 6.6 fusion.2
  499.7 0.0 all-reduce.9.cloned.1.call-update
  499.7 0.0 all-reduce.11.cloned.1.call-start
  499.8 209.7 %all-reduce.9.cloned.1.call-done = f32[2,1024,32]{1,2,0:T(8,128)} async-done(((f32[2,1024,32]{1,2,0:T(8,128)}), f32[2,1024,32]{1,2,0:T(8,128)}) %all-reduce.9.cloned.1.call-update) | async-done | bytes 262160 | tf_op jit(solution)/shard_map/psum | solution.py:31
  709.5 1.4 fusion.12
  710.9 3.6 psum.53
  714.5 0.1 copy.33
  714.6 5.9 custom-call.10
  720.5 0.1 compare_reduce_fusion
  720.6 0.1 select_bitcast_fusion
  720.7 4.9 custom-call.11
  725.6 1.4 fusion.38
  727.0 0.0 copy-start.4
  727.0 5.3 fusion
  732.3 0.0 all-reduce.11.cloned.1.call-update
  732.3 0.0 all-gather.2.cloned.1.call-start
  732.4 2.0 all_gather.6
  734.4 237.4 %all-reduce.11.cloned.1.call-done = f32[2,512,32]{1,2,0:T(8,128)} async-done(((f32[2,512,32]{1,2,0:T(8,128)}), f32[2,512,32]{1,2,0:T(8,128)}) %all-reduce.11.cloned.1.call-update) | async-done | bytes 131088 | tf_op jit(solution)/shard_map/psum | solution.py:35
  971.8 1.0 broadcast_multiply_fusion
  972.8 3.8 fusion.22
  976.5 2.7 gather_fusion
  979.3 0.7 fusion.37
  980.0 0.0 all-gather.2.cloned.1.call-update
  980.1 347.4 %psum.55 = f32[2,1024]{1,0:T(2,128)S(1)} all-reduce(f32[2,1024]{1,0:T(2,128)S(1)} %bitcast.54), channel_id=1, replica_groups=mesh['dp'=128,'sub'=2] {'dp'}, use_global_device_ids=true, to_apply=%region_8.11 | all-reduce | flops 2048 | bytes 16384 | tf_op jit(solution)/shard_map/psum | solution.py:26
  1327.5 0.6 multiply_subtract_fusion
  1328.1 6.1 fusion.9
  1334.2 4.3 gather_fusion.1
  (26 shorter events, 0.2 us)
Async XLA Ops:
  7.2 0.9 copy-start
  7.2 241.3 %copy-start.1 = (bf16[1,2,1024,512]{3,2,1,0:T(8,128)(2,1)S(1)}, bf16[1,2,1024,512]{3,2,1,0:T(8,128)(2,1)}, u32[]{:S(2)}) copy-start(bf16[1,2,1024,512]{3,2,1,0:T(8,128)(2,1)} %param.12) | copy-start | bytes 6291460
  7.2 8.2 copy-start.5
  7.2 223.9 %all-reduce.5.cloned.1.call-start = ((), (), s32[]{:S(2)}) async-start(), calls=%async_computation | async-start | bytes 524288 | tf_op jit(solution)/shard_map/psum | solution.py:31
  15.3 477.8 %all-reduce.7.cloned.1.call-start = ((), (), s32[]{:S(2)}) async-start(), calls=%async_computation.1 | async-start | bytes 262144 | tf_op jit(solution)/shard_map/psum | solution.py:35
  253.7 455.8 %all-reduce.9.cloned.1.call-start = ((), (), s32[]{:S(2)}) async-start(), calls=%async_computation.2 | async-start | bytes 524288 | tf_op jit(solution)/shard_map/psum | solution.py:31
  499.7 472.0 %all-reduce.11.cloned.1.call-start = ((), (), s32[]{:S(2)}) async-start(), calls=%async_computation.3 | async-start | bytes 262144 | tf_op jit(solution)/shard_map/psum | solution.py:35
  727.0 252.3 %copy-start.3 = (f32[4,16,256]{2,1,0:T(8,128)S(1)}, f32[4,16,256]{2,1,0:T(8,128)}, u32[]{:S(2)}) copy-start(f32[4,16,256]{2,1,0:T(8,128)} %param.18) | copy-start | bytes 196612
  727.0 252.3 %copy-start.4 = (f32[4,16,256]{2,1,0:T(8,128)S(1)}, f32[4,16,256]{2,1,0:T(8,128)}, u32[]{:S(2)}) copy-start(f32[4,16,256]{2,1,0:T(8,128)} %param.17) | copy-start | bytes 196612
  727.0 253.1 %copy-start.7 = (f32[1,2,1024]{2,1,0:T(2,128)S(1)}, f32[1,2,1024]{2,1,0:T(2,128)}, u32[]{:S(2)}) copy-start(f32[1,2,1024]{2,1,0:T(2,128)} %param.13) | copy-start | bytes 24580
  727.0 600.5 %copy-start.6 = (f32[2,1024]{1,0:T(2,128)S(1)}, f32[2,1024]{1,0:T(2,128)}, u32[]{:S(2)}) copy-start(f32[2,1024]{1,0:T(2,128)} %param.14) | copy-start | bytes 24580
  732.3 601.9 %all-gather.2.cloned.1.call-start = ((), (), s32[]{:S(2)}) async-start(), calls=%async_computation.4 | async-start | bytes 4227072 | tf_op jit(solution)/shard_map/all_gather | solution.py:59
  971.8 356.3 %copy-start.2 = (f32[2,512,32]{1,2,0:T(8,128)S(1)}, f32[2,512,32]{1,2,0:T(8,128)}, u32[]{:S(2)}) copy-start(f32[2,512,32]{1,2,0:T(8,128)} %all-reduce.11.cloned.1.call-done) | copy-start | bytes 393220
Sparse Core Ops, SparseCore 0:
  15.4 215.6 all-reduce.4
  253.8 239.2 all-reduce.6
  500.0 209.4 all-reduce.8
  732.5 239.2 all-reduce.10
  980.2 113.5 all-gather.1
where the time goes:
time: 1350 us
  waiting for transfers between devices  902 us (67%)
  blocking collectives  356 us (26%)
  matrix products  39.8 us (3%)
  other arithmetic  24.7 us (2%)
  between operations  14 us (1%)
    psum x2, waiting for transfers between devices, body(): right = lax.psum(local_right, ('dp', 'sub')) / replicas  477 us
    psum x2, waiting for transfers between devices, body(): left = lax.psum(local_left, 'dp') / replicas  425 us
    psum x1, blocking collectives, body(): vec_total = lax.psum(vec_grads[0], 'dp')  347 us
  transfers between devices with their start and end apart: 5, of which 4 were waited for; matrix products, arithmetic and copies ran while one was open for 1% of the time, Pallas kernels for 0%

commit v1 on v0

--- a/solution.py
+++ b/solution.py
@@ -1,3 +1,4 @@
+import functools
 import jax
 import jax.numpy as jnp
 from jax import lax
@@ -8,6 +9,14 @@
 momentum_decay = 0.9
 step_rate = 0.5
 vector_rate = 1.0
+
+
+def turn_the_spans(arr_in, named_axis):
+    opened = lax.all_gather(arr_in, axis_name=named_axis)
+    return jnp.sum(opened, axis=0)
+
+
+play_surface = functools.partial(turn_the_spans, named_axis=("dp", "sub"))
 
 
 def solve_basis(left, gram):
@@ -32,7 +41,7 @@
         gram = lax.psum(jnp.einsum("mdr,mds->mrs", left, left, precision=HIGH), "sub")
         basis = solve_basis(left, gram)
         local_right = jnp.einsum("mdk,mdr->mkr", mixed, basis, precision=HIGH)
-        right = lax.psum(local_right, ("dp", "sub")) / replicas
+        right = play_surface(local_right) / replicas
     approx_local = jnp.einsum("mdr,mkr->mdk", basis, right, precision=HIGH)
     errors_out = (mixed - approx_local).astype(jnp.bfloat16)[None]
     basis_full = lax.all_gather(basis.astype(jnp.bfloat16), "sub", axis=1, tiled=True).astype(

time: 1350 us -> 1190 us (0.88)
  waiting for transfers between devices: 902 us -> 723 us
  other arithmetic: 24.7 us -> 47.9 us
    psum x2 -> x0, waiting for transfers between devices: 477 us -> none  [body(): right = lax.psum(local_right, ('dp', 'sub')) / replicas]
    all_gather x0 -> x2, waiting for transfers between devices: none -> 297 us  [turn_the_spans(): opened = lax.all_gather(arr_in, axis_name=named_axis)]
    reduce_sum x0 -> x2, other arithmetic: none -> 24.1 us  [turn_the_spans(): return jnp.sum(opened, axis=0)]
where the time goes in v1:
time: 1190 us
  waiting for transfers between devices  723 us (61%)
  blocking collectives  356 us (30%)
  other arithmetic  47.9 us (4%)
  matrix products  39.7 us (3%)
  between operations  14 us (1%)
    psum x2, waiting for transfers between devices, body(): left = lax.psum(local_left, 'dp') / replicas  426 us
    psum x1, blocking collectives, body(): vec_total = lax.psum(vec_grads[0], 'dp')  347 us
    all_gather x2, waiting for transfers between devices, turn_the_spans(): opened = lax.all_gather(arr_in, axis_name=named_axis)  297 us
    reduce_sum x2, other arithmetic, turn_the_spans(): return jnp.sum(opened, axis=0)  24.1 us
  transfers between devices with their start and end apart: 5, of which 4 were waited for; matrix products, arithmetic and copies ran while one was open for 1% of the time, Pallas kernels for 0%

profile of v1, /device:TPU:2, one launch (start us, length us, event | category | flops | bytes accessed | tf_op | source)
XLA Modules:
  0.0 1189.1 jit_solution(15336198972621357288)
XLA Ops:
  7.2 0.0 copy-start
  7.2 0.0 all-reduce.3.cloned.1.call-start
  7.2 0.8 copy-done
  8.1 7.2 fusion.6
  15.3 0.0 all-reduce.3.cloned.1.call-update
  15.3 0.0 all-gather.8.cloned.1.call-start
  15.4 215.8 %all-reduce.3.cloned.1.call-done = f32[2,1024,32]{1,2,0:T(8,128)} async-done(((f32[2,1024,32]{1,2,0:T(8,128)}), f32[2,1024,32]{1,2,0:T(8,128)}) %all-reduce.3.cloned.1.call-update) | async-done | bytes 262160 | tf_op jit(solution)/shard_map/psum | solution.py:40
  231.2 1.4 fusion.15
  232.6 3.4 psum.36
  236.0 0.1 copy.30
  236.1 5.9 custom-call.8
  242.0 0.1 compare_reduce_fusion.1
  242.1 0.1 select_bitcast_fusion.1
  242.2 4.9 custom-call.9
  247.1 1.4 convolution_bitcast_fusion.1
  248.5 5.2 fusion.4
  253.8 0.0 all-gather.8.cloned.1.call-update
  253.8 0.0 all-reduce.5.cloned.1.call-start
  253.8 149.5 %all-gather.8.cloned.1.call-done = f32[512,512,32]{1,2,0:T(8,128)} async-done(((f32[2,512,32]{1,2,0:T(8,128)}), f32[512,512,32]{1,2,0:T(8,128)}) %all-gather.8.cloned.1.call-update) | async-done | bytes 33554448 | tf_op jit(solution)/shard_map/all_gather | solution.py:15
  403.3 12.1 %reduce_sum.47 = f32[2,512,32]{1,2,0:T(8,128)S(1)} reduce(f32[256,2,512,32]{2,3,1,0:T(8,128)} %bitcast.55, f32[]{:T(128)} %constant.57.clone.1), dimensions={0}, to_apply=%region_4.7 | reduce | flops 8355840 | bytes 33685508 | tf_op jit(solution)/shard_map/reduce_sum | solution.py:16
  415.4 6.6 fusion.2
  422.0 0.0 all-reduce.5.cloned.1.call-update
  422.0 0.2 all-gather.10.cloned.1.call-start
  422.2 210.3 %all-reduce.5.cloned.1.call-done = f32[2,1024,32]{1,2,0:T(8,128)} async-done(((f32[2,1024,32]{1,2,0:T(8,128)}), f32[2,1024,32]{1,2,0:T(8,128)}) %all-reduce.5.cloned.1.call-update) | async-done | bytes 262160 | tf_op jit(solution)/shard_map/psum | solution.py:40
  632.5 1.4 fusion.12
  633.9 3.4 psum.38
  637.3 0.1 copy.33
  637.4 5.9 custom-call.10
  643.3 0.1 compare_reduce_fusion
  643.4 0.1 select_bitcast_fusion
  643.5 4.9 custom-call.11
  648.4 1.4 fusion.38
  649.8 5.2 fusion
  655.1 0.0 all-gather.10.cloned.1.call-update
  655.1 0.0 all-gather.6.cloned.1.call-start
  655.1 0.2 convert_reduce_fusion
  655.3 0.1 convert_reduce_fusion.1
  655.5 2.0 all_gather.22
  657.5 147.1 %all-gather.10.cloned.1.call-done = f32[512,512,32]{1,2,0:T(8,128)} async-done(((f32[2,512,32]{1,2,0:T(8,128)}), f32[512,512,32]{1,2,0:T(8,128)}) %all-gather.10.cloned.1.call-update) | async-done | bytes 33554448 | tf_op jit(solution)/shard_map/all_gather | solution.py:15
  804.6 12.1 %reduce_sum.48 = f32[2,512,32]{1,2,0:T(8,128)S(1)} reduce(f32[256,2,512,32]{2,3,1,0:T(8,128)} %bitcast.54, f32[]{:T(128)} %constant.57.clone.1), dimensions={0}, to_apply=%region_7.10 | reduce | flops 8355840 | bytes 33685508 | tf_op jit(solution)/shard_map/reduce_sum | solution.py:16
  816.7 3.8 fusion.22
  820.5 2.7 gather_fusion
  823.3 0.7 fusion.37
  824.0 0.0 all-gather.6.cloned.1.call-update
  824.1 347.5 %psum.39 = f32[2,1024]{1,0:T(2,128)S(1)} all-reduce(f32[2,1024]{1,0:T(2,128)S(1)} %bitcast.58), channel_id=1, replica_groups=mesh['dp'=128,'sub'=2] {'dp'}, use_global_device_ids=true, to_apply=%region_8.11 | all-reduce | flops 2048 | bytes 16384 | tf_op jit(solution)/shard_map/psum | solution.py:35
  1171.6 0.6 multiply_subtract_fusion
  1172.2 6.1 fusion.9
  1178.3 4.3 gather_fusion.1
  (28 shorter events, 0.2 us)
Async XLA Ops:
  7.2 0.9 copy-start
  7.2 241.3 %copy-start.2 = (bf16[1,2,1024,512]{3,2,1,0:T(8,128)(2,1)S(1)}, bf16[1,2,1024,512]{3,2,1,0:T(8,128)(2,1)}, u32[]{:S(2)}) copy-start(bf16[1,2,1024,512]{3,2,1,0:T(8,128)(2,1)} %param.12) | copy-start | bytes 6291460
  7.2 224.0 %all-reduce.3.cloned.1.call-start = ((), (), s32[]{:S(2)}) async-start(), calls=%async_computation | async-start | bytes 524288 | tf_op jit(solution)/shard_map/psum | solution.py:40
  15.3 388.0 %all-gather.8.cloned.1.call-start = ((), (), s32[]{:S(2)}) async-start(), calls=%async_computation.3 | async-start | bytes 33685504 | tf_op jit(solution)/shard_map/all_gather | solution.py:15
  253.8 378.7 %all-reduce.5.cloned.1.call-start = ((), (), s32[]{:S(2)}) async-start(), calls=%async_computation.1 | async-start | bytes 524288 | tf_op jit(solution)/shard_map/psum | solution.py:40
  422.0 233.2 %copy-start.5 = (s32[256]{0:T(256)S(1)}, s32[256]{0:T(256)}, u32[]{:S(2)}) copy-start(s32[256]{0:T(256)} %param.16) | copy-start | bytes 3076
  422.0 382.6 %all-gather.10.cloned.1.call-start = ((), (), s32[]{:S(2)}) async-start(), calls=%async_computation.4 | async-start | bytes 33685504 | tf_op jit(solution)/shard_map/all_gather | solution.py:15
  655.1 523.2 %all-gather.6.cloned.1.call-start = ((), (), s32[]{:S(2)}) async-start(), calls=%async_computation.2 | async-start | bytes 4227072 | tf_op jit(solution)/shard_map/all_gather | solution.py:68
  816.7 6.6 copy-start.3
  816.7 6.6 copy-start.4
  816.7 7.4 copy-start.7
  816.7 354.8 %copy-start.6 = (f32[2,1024]{1,0:T(2,128)S(1)}, f32[2,1024]{1,0:T(2,128)}, u32[]{:S(2)}) copy-start(f32[2,1024]{1,0:T(2,128)} %param.14) | copy-start | bytes 24580
  1171.6 11.0 copy-start.1
Sparse Core Ops, SparseCore 0:
  15.4 215.7 all-reduce.2
  253.9 149.3 all-gather.7
  422.1 210.3 all-reduce.4
  655.2 149.3 all-gather.9
  824.2 114.4 all-gather.5
